TPU v7x, 32 devices: a whole 2x2x4 slice. The times are simulated.
32 devices in a mesh: groups: 2 (over x), seq: 16 (over z, y, core).
Axes of the slice: x: 2, y: 2, z: 4, core: 2. Of those that a mesh axis runs over, the one named last changes fastest.
Arguments:
- queries: bfloat16 [4096, 2048], P(('groups', 'seq')), parts along dimension 0, may hold values from -140 to 140
- keys: bfloat16 [4096, 2048], P(('groups', 'seq')), parts along dimension 0, may hold values from -6.25 to 6.25
- values: bfloat16 [4096, 2048], P(('groups', 'seq')), parts along dimension 0, may hold values from -6 to 6
- grad_out: bfloat16 [4096, 2048], P(('groups', 'seq')), parts along dimension 0, may hold values from -6 to 6
- partners: int32 [32, 16, 3], P(('groups', 'seq')), parts along dimension 0, may hold values from 0 to 15, all different within a row; in each aligned block of 16 rows (0 to 15, 16 to 31, ..., all dimensions but the last counted through in order) at most 3 rows name the same one
Outputs:
- grad_queries: bfloat16 [4096, 2048], P(('groups', 'seq')), parts along dimension 0
- grad_keys: bfloat16 [4096, 2048], P(('groups', 'seq')), parts along dimension 0
- grad_values: bfloat16 [4096, 2048], P(('groups', 'seq')), parts along dimension 0
There are 2 independent parts, one for each index of `groups`. A program takes and returns all parts, laid end to end along the dimension named above; each array names one. Nothing has to cross between parts.
Inputs may be any that keep to these rules, and one draw needn't show every extreme that they name: In the 16 head rows of one query block, no block is named more than 3 times, and some block is named exactly 3 times; the 3 partners of one head are different blocks.
All inputs are finite; a program needn't handle non-finite values.
Results may differ from a plain program's by a relative error of at most 0.01.
Values may be sent and summed in bfloat16 or wider, within the bound.
A program may use at most 128 MiB of HBM per device.

v0:
```python
import math
import jax
import jax.numpy as jnp
from jax import lax
from jax.sharding import PartitionSpec as P

H = 16
HD = 128


def with_halo(shard, sides, width):
    for axis, dim in sides:
        count, length = (lax.axis_size(axis), shard.shape[dim])
        up = [(i, (i + 1) % count) for i in range(count - 1)]
        down = [(j, i) for i, j in up]
        last = lax.slice_in_dim(shard, length - width, length, axis=dim)
        first = lax.slice_in_dim(shard, 0, width, axis=dim)
        before = lax.ppermute(last, axis, up)
        after = lax.ppermute(first, axis, down)
        shard = jnp.concatenate([before, shard, after], axis=dim)
    return shard


def broadcast(block, axis, source):
    block = jnp.where(lax.axis_index(axis) == source, block, jnp.zeros_like(block))
    return lax.psum(block, axis)


def per_device(queries, keys, values, grad_out, partners):
    devices = lax.axis_size("seq")
    my_index = lax.axis_index("seq")
    most_slots = max(2, (3 * H + devices - 1) // devices)
    softmax_scale = 1.0 / math.sqrt(HD)
    width = H * HD
    rows_here = queries.shape[0]
    kv_local = jnp.stack([keys, values])
    query_heads = queries.reshape(rows_here, H, HD)
    grad_heads = grad_out.reshape(rows_here, H, HD)
    lower_ok = my_index > 0
    upper_ok = my_index < devices - 1
    window = with_halo(kv_local, (("seq", 1),), rows_here)
    sink_parts = [broadcast(kv_local, "seq", sink_root) for sink_root in range(2)]
    near_kv = jnp.concatenate([window] + sink_parts, axis=1).reshape(2, 5 * rows_here, H, HD)
    near_keys = near_kv[0]
    near_values = near_kv[1]
    item_count = 3 * H
    dests = partners.reshape(item_count)
    item_heads = jnp.arange(item_count, dtype=jnp.int32) // 3
    dest_hot = (dests[:, None] == jnp.arange(devices, dtype=jnp.int32)[None, :]).astype(jnp.int32)
    slot_rank = jnp.sum((jnp.cumsum(dest_hot, axis=0) - dest_hot) * dest_hot, axis=1)
    kv_by_head = kv_local.reshape(2, rows_here, H, HD).transpose(2, 0, 1, 3)
    requests = jnp.full((devices, most_slots), -1, jnp.int32).at[dests, slot_rank].set(item_heads)
    wanted = lax.all_to_all(requests, "seq", split_axis=0, concat_axis=0, tiled=True)
    picked = kv_by_head[jnp.maximum(wanted, 0)]
    fetched = lax.all_to_all(
        jnp.where((wanted >= 0)[:, :, None, None, None], picked, jnp.zeros_like(picked)),
        "seq",
        split_axis=0,
        concat_axis=0,
        tiled=True,
    )
    far_kv = fetched[dests, slot_rank].reshape(H, 3, 2, rows_here, HD)
    far_keys = far_kv[:, :, 0]
    far_values = far_kv[:, :, 1]
    near_scores = softmax_scale * jnp.einsum(
        "thd,khd->htk", query_heads, near_keys, preferred_element_type=jnp.float32
    )
    far_scores = softmax_scale * jnp.einsum(
        "thd,hrkd->htrk", query_heads, far_keys, preferred_element_type=jnp.float32
    )
    key_pos = jnp.arange(5 * rows_here, dtype=jnp.int32)
    key_ok = jnp.logical_not((key_pos < rows_here) & jnp.logical_not(lower_ok))
    key_ok = key_ok & jnp.logical_not(
        (key_pos >= 2 * rows_here) & (key_pos < 3 * rows_here) & jnp.logical_not(upper_ok)
    )
    near_max = jnp.max(
        jnp.where(key_ok[None, None, :], near_scores, -jnp.inf), axis=2, keepdims=True
    )
    far_max = jnp.max(far_scores, axis=(2, 3))[:, :, None]
    row_max = jnp.maximum(near_max, far_max)
    near_total = jnp.sum(
        jnp.where(key_ok[None, None, :], jnp.exp(near_scores - row_max), 0.0), axis=2, keepdims=True
    )
    far_total = jnp.sum(jnp.exp(far_scores - row_max[:, :, :, None]), axis=(2, 3))[:, :, None]
    totals = near_total + far_total

    def near_prob_f32():
        return jnp.where(key_ok[None, None, :], jnp.exp(near_scores - row_max), 0.0) / totals

    def far_prob_f32():
        return jnp.exp(far_scores - row_max[:, :, :, None]) / totals[:, :, :, None]

    near_probs = near_prob_f32().astype(jnp.bfloat16)
    far_probs = far_prob_f32().astype(jnp.bfloat16)
    attended = jnp.einsum(
        "htk,khd->htd", near_probs, near_values, preferred_element_type=jnp.float32
    )
    attended = attended + jnp.einsum(
        "htrk,hrkd->htd", far_probs, far_values, preferred_element_type=jnp.float32
    )
    delta = jnp.sum(grad_heads.transpose(1, 0, 2) * attended, axis=2)
    near_dprob = jnp.einsum(
        "thd,khd->htk", grad_heads, near_values, preferred_element_type=jnp.float32
    )
    far_dprob = jnp.einsum(
        "thd,hrkd->htrk", grad_heads, far_values, preferred_element_type=jnp.float32
    )
    near_dscore = (near_prob_f32() * (near_dprob - delta[:, :, None])).astype(jnp.bfloat16)
    far_dscore = (far_prob_f32() * (far_dprob - delta[:, :, None, None])).astype(jnp.bfloat16)
    grad_q = jnp.einsum("htk,khd->thd", near_dscore, near_keys, preferred_element_type=jnp.float32)
    grad_q = grad_q + jnp.einsum(
        "htrk,hrkd->thd", far_dscore, far_keys, preferred_element_type=jnp.float32
    )
    grad_queries = (softmax_scale * grad_q).reshape(rows_here, width).astype(jnp.bfloat16)
    near_key_term = softmax_scale * jnp.einsum(
        "htk,thd->khd", near_dscore, query_heads, preferred_element_type=jnp.float32
    )
    near_value_term = jnp.einsum(
        "htk,thd->khd", near_probs, grad_heads, preferred_element_type=jnp.float32
    )
    near_terms = jnp.stack(
        [near_key_term.reshape(5 * rows_here, width), near_value_term.reshape(5 * rows_here, width)]
    )
    own_grads = near_terms[:, rows_here : 2 * rows_here]
    outgoing = jnp.concatenate(
        [near_terms[:, :rows_here], near_terms[:, 2 * rows_here : 3 * rows_here]], axis=1
    )
    incoming = with_halo(outgoing.astype(jnp.bfloat16), (("seq", 1),), rows_here).astype(
        outgoing.dtype
    )
    own_grads = own_grads + incoming[:, :rows_here] + incoming[:, 3 * rows_here :]
    sink_terms = (
        near_terms[:, 3 * rows_here :].reshape(2, 2, rows_here, width).transpose(1, 0, 2, 3)
    )
    sink_total = lax.psum(sink_terms, "seq")
    sink_mine = lax.dynamic_index_in_dim(sink_total, jnp.minimum(my_index, 1), 0, keepdims=False)
    own_grads = own_grads + jnp.where(my_index < 2, sink_mine, jnp.zeros_like(sink_mine))
    far_key_term = softmax_scale * jnp.einsum(
        "htrk,thd->hrkd", far_dscore, query_heads, preferred_element_type=jnp.float32
    )
    far_value_term = jnp.einsum(
        "htrk,thd->hrkd", far_probs, grad_heads, preferred_element_type=jnp.float32
    )
    far_terms = (
        jnp.stack([far_key_term, far_value_term], axis=2)
        .astype(jnp.bfloat16)
        .reshape(item_count, 2, rows_here, HD)
    )
    outbox = (
        jnp.zeros((devices, most_slots, 2, rows_here, HD), jnp.bfloat16)
        .at[dests, slot_rank]
        .set(far_terms)
    )
    returned = lax.all_to_all(outbox, "seq", split_axis=0, concat_axis=0, tiled=True)
    head_hot = (wanted[:, :, None] == jnp.arange(H, dtype=jnp.int32)[None, None, :]).astype(
        jnp.bfloat16
    )
    gained = jnp.einsum("nmh,nmcbd->cbhd", head_hot, returned, preferred_element_type=jnp.float32)
    own_grads = own_grads + gained.reshape(2, rows_here, width)
    return (grad_queries, own_grads[0].astype(jnp.bfloat16), own_grads[1].astype(jnp.bfloat16))


def solution(mesh):
    placed = (
        P(("groups", "seq"), None),
        P(("groups", "seq"), None),
        P(("groups", "seq"), None),
        P(("groups", "seq"), None),
        P(("groups", "seq"), None, None),
    )
    return jax.shard_map(
        per_device,
        mesh=mesh,
        in_specs=placed,
        out_specs=(
            P(("groups", "seq"), None),
            P(("groups", "seq"), None),
            P(("groups", "seq"), None),
        ),
        check_vma=False,
    )
```

profile of v0, /device:TPU:0, one launch (start us, length us, event | category | flops | bytes accessed | tf_op | source)
XLA Modules:
  0.0 459.0 jit_solution(7758403241742781614)
XLA Ops:
  8.5 2.8 scatter_fusion
  12.0 7.4 %all-to-all-start = ((s32[16,1,3]{2,1,0:T(1,128)}), s32[16,1,3]{2,1,0:T(1,128)S(1)}, u32[]{:S(2)}, u32[]{:S(2)}) async-start(s32[16,1,3]{2,1,0:T(1,128)} %copy.159), calls=%async_computation | async-start | bytes 16384 | tf_op jit(solution)/shard_map/all_to_all | solution.py:53
  19.4 1.3 copy.154
  21.7 4.0 all-to-all-done
  26.0 2.7 gather_fusion
  28.7 3.8 broadcast_select_fusion
  32.5 4.5 all-to-all-start.1
  37.2 2.2 collective-permute-start
  39.4 1.5 collective-permute-start.1
  41.8 2.0 broadcast_select_fusion.1
  43.8 2.3 copy-done.6
  47.3 1.2 copy.179
  48.5 2.4 constant_dynamic-update-slice_fusion.2
  50.9 169.4 %all-reduce.6.cloned.1.call-done = (bf16[2,128,2048]{1,2,0:T(8,128)(2,1)}, bf16[2,128,2048]{1,2,0:T(8,128)(2,1)}) async-done(((bf16[2,128,2048]{1,2,0:T(8,128)(2,1)}, bf16[2,128,2048]{1,2,0:T(8,128)(2,1)}), (bf16[2,128,2048]{1,2,0:T(8,128)(2,1)}, bf16[2,128,2048]{1,2,0:T(8,128)(2,1)})) %all-reduce.6.cloned.1.call-update) | async-done | bytes 2097168 | tf_op jit(solution)/shard_map/psum | solution.py:26
  220.3 2.4 constant_dynamic-update-slice_fusion.1
  222.7 2.3 constant_dynamic-update-slice_fusion
  225.0 4.6 %fusion.52 = (bf16[1,640,2048]{1,2,0:T(8,128)(2,1)}, bf16[1,640,2048]{1,2,0:T(8,128)(2,1)S(1)}) fusion(bf16[2,640,2048]{1,2,0:T(8,128)(2,1)} %constant_dynamic-update-slice_fusion), kind=kLoop, calls=%fused_computation.102 | loop fusion | bytes 10485760 | tf_op jit(solution)/shard_map/slice | solution.py:45
  229.6 3.7 select_reduce_fusion
  233.3 4.7 %gather_fusion.1 = bf16[48,2,128,128]{3,2,1,0:T(8,128)(2,1)} fusion(bf16[16,3,2,128,128]{4,3,2,1,0:T(8,128)(2,1)} %all-to-all-done.1, s32[48]{0:T(128)S(1)} %bitcast.171), kind=kCustom, calls=%fused_computation.1 | custom fusion | bytes 6291840 | tf_op jit(solution)/shard_map/gather | solution.py:62
  238.0 2.1 copy.166
  240.7 3.0 copy-done.2
  243.7 1.1 bitcast_reduce_fusion
  245.4 1.1 fusion.21
  248.2 1.8 fusion.29
  252.2 2.2 pad_maximum_fusion.1
  254.3 2.5 broadcast.125
  256.9 9.6 %scatter_fusion.1 = bf16[16,3,2,128,128]{4,3,2,1,0:T(8,128)(2,1)} fusion(bf16[16,3,2,128,128]{4,3,2,1,0:T(8,128)(2,1)} %broadcast.125, s32[48]{0:T(128)S(1)} %get-tuple-element.20, bf16[48,2,128,128]{3,2,1,0:T(8,128)(2,1)} %pad_maximum_fusion.1), kind=kCustom, calls=%fused_computation.3 | custom fusion | bytes 9437568 | tf_op jit(solution)/shard_map/scatter | solution.py:152
  266.4 4.5 all-to-all-start.2
  271.0 5.7 %fusion.1 = bf16[16,128,640]{1,2,0:T(8,128)(2,1)S(1)} fusion(f32[16,128]{1,0:T(8,128)S(1)} %fusion.29, bf16[640,16,128]{0,2,1:T(8,128)(2,1)} %bitcast.167, bf16[128,16,128]{0,2,1:T(8,128)(2,1)} %bitcast.173, f32[16,128]{1,0:T(8,128)S(1)} %add.70, f32[16,128]{1,0:T(8,128)S(1)} %max.27, f32[16,640,128]{2,1,0:T(8,128)} %get-tuple-element.32, ...), kind=kOutput, calls=%fused_computation.11 | convolution fusion | flops 344719360 | bytes 11035264 | tf_op jit(solution)/shard_map/thd,khd->htk/dot_general | solution.py:102
  276.7 1.6 copy-done.4
  278.3 3.2 multiply_bitcast_fusion
  281.5 6.0 %copy.181 = f32[640,16,128]{0,2,1:T(8,128)} copy(f32[640,16,128]{2,0,1:T(8,128)} %multiply_bitcast_fusion) | data formatting | bytes 10485760 | tf_op jit(solution)/shard_map/mul | solution.py:115
  287.4 4.1 fusion.25
  291.6 2.3 copy-done.1
  293.9 2.3 fusion.2
  296.2 5.4 %copy.183 = f32[2,256,2048]{2,1,0:T(8,128)} copy(f32[2,256,2048]{1,2,0:T(8,128)} %fusion.2) | data formatting | bytes 8388608 | tf_op jit(solution)/shard_map/slice | solution.py:133
  301.6 5.3 %copy.184 = f32[2,2,128,2048]{2,3,0,1:T(8,128)} copy(f32[2,2,128,2048]{3,2,1,0:T(8,128)} %bitcast.151) | data formatting | bytes 8388608 | tf_op jit(solution)/shard_map/reshape | solution.py:133
  307.0 4.8 %fusion = bf16[2,640,2048]{1,2,0:T(8,128)(2,1)S(1)} fusion(f32[1,640,2048]{1,2,0:T(8,128)} %bitcast.146, f32[1,640,2048]{1,2,0:T(8,128)} %bitcast.142), kind=kLoop, calls=%fused_computation.9 | loop fusion | flops 2621440 | bytes 15728640 | tf_op jit(solution)/shard_map/convert.9
  311.8 1.7 fusion.51
  313.4 1.3 collective-permute-start.3
  314.7 4.0 collective-permute-start.2
  318.7 2.8 fusion.22
  323.4 14.6 %all-to-all-done.2 = bf16[16,3,2,128,128]{4,3,2,1,0:T(8,128)(2,1)} async-done(((bf16[16,3,2,128,128]{4,3,2,1,0:T(8,128)(2,1)}), bf16[16,3,2,128,128]{4,3,2,1,0:T(8,128)(2,1)}, u32[]{:S(2)}, u32[]{:S(2)}) %all-to-all-start.2) | async-done | bytes 3145760 | tf_op jit(solution)/shard_map/all_to_all | solution.py:154
  338.0 5.0 %fusion.15 = f32[2,128,16,128]{3,2,1,0:T(8,128)} fusion(bf16[16,3,2,128,128]{4,3,2,1,0:T(8,128)(2,1)} %all-to-all-done.2, s32[16,3]{0,1:T(4,128)S(1)} %bitcast.178), kind=kOutput, calls=%fused_computation.37 | convolution fusion | flops 50332416 | bytes 5243072 | tf_op jit(solution)/shard_map/nmh,nmcbd->cbhd/dot_general | solution.py:158
  343.0 2.0 copy.222
  345.1 101.8 %all-reduce.4.cloned.1.call-done = f32[2,2,128,2048]{2,3,1,0:T(8,128)} async-done(((f32[2,2,128,2048]{2,3,1,0:T(8,128)}), f32[2,2,128,2048]{2,3,1,0:T(8,128)}) %all-reduce.4.cloned.1.call-update) | async-done | bytes 4194320 | tf_op jit(solution)/shard_map/psum | solution.py:135
  446.9 3.2 fusion.14
  450.1 1.0 copy.192
  (73 shorter events, 13.6 us)
Async XLA Ops:
  7.2 13.8 %copy-start.11 = (bf16[128,2048]{1,0:T(8,128)(2,1)S(1)}, bf16[128,2048]{1,0:T(8,128)(2,1)}, u32[]{:S(2)}) copy-start(bf16[128,2048]{1,0:T(8,128)(2,1)} %param.6) | copy-start | bytes 1572868
  12.0 13.7 %all-to-all-start = ((s32[16,1,3]{2,1,0:T(1,128)}), s32[16,1,3]{2,1,0:T(1,128)S(1)}, u32[]{:S(2)}, u32[]{:S(2)}) async-start(s32[16,1,3]{2,1,0:T(1,128)} %copy.159), calls=%async_computation | async-start | bytes 16384 | tf_op jit(solution)/shard_map/all_to_all | solution.py:53
  32.5 200.8 %all-to-all-start.1 = ((bf16[16,3,2,128,128]{4,3,2,1,0:T(8,128)(2,1)}), bf16[16,3,2,128,128]{4,3,2,1,0:T(8,128)(2,1)}, u32[]{:S(2)}, u32[]{:S(2)}) async-start(bf16[16,3,2,128,128]{4,3,2,1,0:T(8,128)(2,1)} %broadcast_select_fusion), calls=%async_computation.1 | async-start | bytes 6291456 | tf_op jit(solution)/shard_map/all_to_all | solution.py:55
  37.0 183.3 %all-reduce.6.cloned.1.call-start = ((), (), s32[]{:S(2)}) async-start(), calls=%async_computation.4 | async-start | bytes 4194304 | tf_op jit(solution)/shard_map/psum | solution.py:26
  37.2 4.4 collective-permute-start
  39.4 9.1 %collective-permute-start.1 = (bf16[2,128,2048]{1,2,0:T(8,128)(2,1)S(1)}, bf16[2,128,2048]{1,2,0:T(8,128)(2,1)}, u32[]{:S(2)}, u32[]{:S(2)}) collective-permute-start(bf16[2,128,2048]{1,2,0:T(8,128)(2,1)S(1)} %pad_maximum_fusion.5), channel_id=1, source_target_pairs={{1,0},{2,1},{3,2},{4,3},{5,4},{6,5},{7,6},{8,7},{9,8},{10,9},{11,1... | collective-permute-start | bytes 3145736 | tf_op jit(solution)/shard_map/ppermute | solution.py:19
  41.8 4.3 copy-start.12
  43.8 2.3 copy-start.6
  46.1 1.0 copy-start.13
  225.0 4.6 %copy-start.8 = (bf16[128,16,128]{0,2,1:T(8,128)(2,1)S(1)}, bf16[128,16,128]{0,2,1:T(8,128)(2,1)}, u32[]{:S(2)}) copy-start(bf16[128,16,128]{0,2,1:T(8,128)(2,1)} %copy.179) | copy-start | bytes 1572868
  240.1 10.0 %copy-start.3 = (bf16[48,2,128,128]{3,2,0,1:T(8,128)(2,1)}, bf16[48,2,128,128]{3,2,0,1:T(8,128)(2,1)S(1)}, u32[]{:S(2)}) copy-start(bf16[48,2,128,128]{3,2,0,1:T(8,128)(2,1)S(1)} %copy.166) | copy-start | bytes 9437188
  240.1 3.6 copy-start.2
  245.4 1.1 copy-start.14
  246.5 1.7 copy-start.10
  251.0 1.1 copy-start.7
  266.4 71.6 %all-to-all-start.2 = ((bf16[16,3,2,128,128]{4,3,2,1,0:T(8,128)(2,1)}), bf16[16,3,2,128,128]{4,3,2,1,0:T(8,128)(2,1)}, u32[]{:S(2)}, u32[]{:S(2)}) async-start(bf16[16,3,2,128,128]{4,3,2,1,0:T(8,128)(2,1)} %scatter_fusion.1), calls=%async_computation.2 | async-start | bytes 6291456 | tf_op jit(solution)/shard_map/all_to_all | solution.py:154
  270.9 7.4 %copy-start.9 = (bf16[128,16,128]{0,2,1:T(8,128)(2,1)S(1)}, bf16[128,16,128]{0,2,1:T(8,128)(2,1)}, u32[]{:S(2)}) copy-start(bf16[128,16,128]{0,2,1:T(8,128)(2,1)} %copy.179) | copy-start | bytes 1572868
  270.9 175.9 %all-reduce.4.cloned.1.call-start = ((), (), s32[]{:S(2)}) async-start(), calls=%async_computation.3 | async-start | bytes 8388608 | tf_op jit(solution)/shard_map/psum | solution.py:135
  276.7 1.6 copy-start.4
  281.5 6.0 %copy-start.15 = (bf16[128,2048]{0,1:T(8,128)(2,1)S(1)}, bf16[128,2048]{0,1:T(8,128)(2,1)}, u32[]{:S(2)}) copy-start(bf16[128,2048]{0,1:T(8,128)(2,1)} %copy.168) | copy-start | bytes 1572868
  287.4 6.5 %copy-start = (f32[640,16,128]{0,2,1:T(8,128)S(1)}, f32[640,16,128]{0,2,1:T(8,128)}, u32[]{:S(2)}) copy-start(f32[640,16,128]{0,2,1:T(8,128)} %copy.181) | copy-start | bytes 15728644
  291.6 2.3 copy-start.1
  313.4 31.7 %collective-permute-start.3 = (bf16[2,128,2048]{1,2,0:T(8,128)(2,1)}, bf16[2,128,2048]{1,2,0:T(8,128)(2,1)}, u32[]{:S(2)}, u32[]{:S(2)}) collective-permute-start(bf16[2,128,2048]{1,2,0:T(8,128)(2,1)} %get-tuple-element.23), channel_id=1, source_target_pairs={{1,0},{2,1},{3,2},{4,3},{5,4},{6,5},{7,6},{8,7},{9,8},{10,9},{11,1... | collective-permute-start | bytes 3145736 | tf_op jit(solution)/shard_map/ppermute | solution.py:19
  314.7 30.4 %collective-permute-start.2 = (bf16[2,128,2048]{1,2,0:T(8,128)(2,1)}, bf16[2,128,2048]{1,2,0:T(8,128)(2,1)}, u32[]{:S(2)}, u32[]{:S(2)}) collective-permute-start(bf16[2,128,2048]{1,2,0:T(8,128)(2,1)} %get-tuple-element.22), channel_id=1, source_target_pairs={{0,1},{1,2},{2,3},{3,4},{4,5},{5,6},{6,7},{7,8},{8,9},{9,10},{10,1... | collective-permute-start | bytes 3145736 | tf_op jit(solution)/shard_map/ppermute | solution.py:18
  318.7 2.8 copy-start.5
Sparse Core Ops, SparseCore 0:
  46.2 173.9 all-reduce.5
  307.1 139.7 all-reduce.3
where the time goes:
time: 460 us; the launch traced here: 459 us
  waiting for transfers between devices  291 us (63%)
  local copies, waits for them, and re-layouts  76.9 us (17%)
  matrix products  31.2 us (7%)
  starting transfers between devices  25.4 us (6%)
  other arithmetic  20.4 us (4%)
  between operations  14.5 us (3%)
    psum x1, waiting for transfers between devices, broadcast(): return lax.psum(block, axis)  169 us
    psum x1, waiting for transfers between devices, per_device(): sink_total = lax.psum(sink_terms, 'seq')  102 us
    unnamed x43, local copies, waits for them, and re-layouts  22.3 us
    all_to_all x1, waiting for transfers between devices, per_device(): lax.all_to_all(outbox, 'seq', split_axis=0, concat_axis=0, tiled=True)  14.6 us
    scatter x1, local copies, waits for them, and re-layouts, per_device(): outbox = jnp.zeros((devices, most_slots, 2, rows_here, HD), jnp.bfloat16)...  9.56 us
  transfers between devices with their start and end apart: 9, of which 5 were waited for; matrix products, arithmetic and copies ran while one was open for 16% of the time, Pallas kernels for 0%

commit v1 on v0

--- a/solution.py
+++ b/solution.py
@@ -132,7 +132,11 @@
     sink_terms = (
         near_terms[:, 3 * rows_here :].reshape(2, 2, rows_here, width).transpose(1, 0, 2, 3)
     )
-    sink_total = lax.psum(sink_terms, "seq")
+    sink_total = sink_terms
+    for hop in (1, 2, 4, 8):
+        sink_total = sink_total + lax.ppermute(
+            sink_total, "seq", [(dev, dev ^ hop) for dev in range(16)]
+        )
     sink_mine = lax.dynamic_index_in_dim(sink_total, jnp.minimum(my_index, 1), 0, keepdims=False)
     own_grads = own_grads + jnp.where(my_index < 2, sink_mine, jnp.zeros_like(sink_mine))
     far_key_term = softmax_scale * jnp.einsum(

time: 460 us -> 728 us (1.58); the launches traced: 459 us -> 714 us
  waiting for transfers between devices: 291 us -> 533 us
  other arithmetic: 20.4 us -> 35.1 us
    ppermute x0 -> x4, waiting for transfers between devices: none -> 367 us  [per_device(): lax.ppermute(sink_total, 'seq', [(dev, dev ^ hop) for dev in range(16)])]
    psum x1 -> x0, waiting for transfers between devices: 102 us -> none  [per_device(): sink_total = lax.psum(sink_terms, 'seq')]
    all_to_all x1, waiting for transfers between devices: 14.6 us -> 0.01 us  [per_device(): lax.all_to_all(outbox, 'seq', split_axis=0, concat_axis=0, tiled=True)]
    add x0 -> x3, other arithmetic: none -> 11 us  [per_device(): sink_total + lax.ppermute(sink_total, 'seq', [(dev, dev ^ hop) for dev in...]
    unnamed x43 -> x49, local copies, waits for them, and re-layouts: 22.3 us -> 23.5 us
  transfers between devices with their start and end apart: 9 -> 12, of which waited for: 5 -> 7; matrix products, arithmetic and copies ran while one was open for 16% -> 10% of each run, Pallas kernels for 0% -> 0%
where the time goes in v1:
time: 728 us; the launch traced here: 714 us
  waiting for transfers between devices  533 us (73%)
  local copies, waits for them, and re-layouts  76.3 us (10%)
  other arithmetic  35.1 us (5%)
  matrix products  28.3 us (4%)
  starting transfers between devices  27.3 us (4%)
  between operations  14.5 us (2%)
    ppermute x4, waiting for transfers between devices, per_device(): lax.ppermute(sink_total, 'seq', [(dev, dev ^ hop) for dev in range(16)])  367 us
    psum x1, waiting for transfers between devices, broadcast(): return lax.psum(block, axis)  163 us
    unnamed x49, local copies, waits for them, and re-layouts  23.5 us
  transfers between devices with their start and end apart: 12, of which 7 were waited for; matrix products, arithmetic and copies ran while one was open for 10% of the time, Pallas kernels for 0%

profile of v1, /device:TPU:0, one launch (start us, length us, event | category | flops | bytes accessed | tf_op | source)
XLA Modules:
  0.0 714.0 jit_solution(15323161575644097534)
XLA Ops:
  8.5 2.8 scatter_fusion
  11.9 7.4 %all-to-all-start = ((s32[16,1,3]{2,1,0:T(1,128)}), s32[16,1,3]{2,1,0:T(1,128)S(1)}, u32[]{:S(2)}, u32[]{:S(2)}) async-start(s32[16,1,3]{2,1,0:T(1,128)} %copy.159), calls=%async_computation | async-start | bytes 16384 | tf_op jit(solution)/shard_map/all_to_all | solution.py:53
  23.4 2.3 all-to-all-done
  26.0 2.7 gather_fusion
  28.7 3.8 broadcast_select_fusion
  32.5 3.7 all-to-all-start.1
  36.3 2.3 pad_maximum_fusion.5
  38.6 3.3 collective-permute-start
  43.5 2.4 constant_dynamic-update-slice_fusion.4
  45.9 3.4 broadcast_select_fusion.1
  49.3 2.0 copy.223
  51.3 2.2 copy.179
  53.5 2.0 copy.168
  55.6 2.3 constant_dynamic-update-slice_fusion.2
  57.9 163.3 %all-reduce.3.cloned.1.call-done = (bf16[2,128,2048]{1,2,0:T(8,128)(2,1)}, bf16[2,128,2048]{1,2,0:T(8,128)(2,1)}) async-done(((bf16[2,128,2048]{1,2,0:T(8,128)(2,1)}, bf16[2,128,2048]{1,2,0:T(8,128)(2,1)}), (bf16[2,128,2048]{1,2,0:T(8,128)(2,1)}, bf16[2,128,2048]{1,2,0:T(8,128)(2,1)})) %all-reduce.3.cloned.1.call-update) | async-done | bytes 2097168 | tf_op jit(solution)/shard_map/psum | solution.py:26
  221.2 2.3 constant_dynamic-update-slice_fusion.1
  223.5 2.4 constant_dynamic-update-slice_fusion
  225.9 4.5 fusion.54
  230.4 1.6 copy-done
  232.0 3.7 select_reduce_fusion
  235.8 2.8 gather_fusion.1
  238.6 2.4 copy.166
  245.5 3.8 fusion.27
  249.4 2.0 fusion.31
  251.3 2.7 fusion.1
  255.5 3.2 multiply_bitcast_fusion
  258.7 6.0 copy.181
  264.7 4.5 fusion.2
  269.1 5.3 copy.183
  274.5 5.3 copy.184
  279.8 7.4 %collective-permute-done.4 = f32[2,2,128,2048]{2,3,1,0:T(8,128)S(1)} collective-permute-done((f32[2,2,128,2048]{2,3,1,0:T(8,128)}, f32[2,2,128,2048]{2,3,1,0:T(8,128)S(1)}, u32[]{:S(2)}, u32[]{:S(2)}) %collective-permute-start.4) | collective-permute-done | bytes 4194336 | tf_op jit(solution)/shard_map/ppermute | solution.py:137
  287.2 2.8 bitcast_add_fusion
  291.1 91.6 %collective-permute-done.5 = f32[2,2,128,2048]{2,3,1,0:T(8,128)S(1)} collective-permute-done((f32[2,2,128,2048]{2,3,1,0:T(8,128)S(1)}, f32[2,2,128,2048]{2,3,1,0:T(8,128)S(1)}, u32[]{:S(2)}, u32[]{:S(2)}) %collective-permute-start.5) | collective-permute-done | bytes 4194336 | tf_op jit(solution)/shard_map/ppermute | solution.py:137
  382.7 2.4 add.86
  390.5 2.5 broadcast.125
  393.0 8.5 %scatter_fusion.1 = bf16[16,3,2,128,128]{4,3,2,1,0:T(8,128)(2,1)} fusion(bf16[16,3,2,128,128]{4,3,2,1,0:T(8,128)(2,1)} %broadcast.125, s32[48]{0:T(128)S(1)} %get-tuple-element.20, bf16[48,2,128,128]{3,2,1,0:T(8,128)(2,1)S(1)} %pad_maximum_fusion.1), kind=kCustom, calls=%fused_computation.3 | custom fusion | bytes 9437568 | tf_op jit(solution)/shard_map/scatter | solution.py:156
  401.5 4.6 all-to-all-start.2
  406.1 105.0 %collective-permute-done.6 = f32[2,2,128,2048]{2,3,1,0:T(8,128)} collective-permute-done((f32[2,2,128,2048]{2,3,1,0:T(8,128)}, f32[2,2,128,2048]{2,3,1,0:T(8,128)}, u32[]{:S(2)}, u32[]{:S(2)}) %collective-permute-start.6) | collective-permute-done | bytes 4194336 | tf_op jit(solution)/shard_map/ppermute | solution.py:137
  511.2 5.8 add.87
  517.0 3.2 fusion
  520.2 1.7 fusion.53
  521.9 2.5 collective-permute-start.2
  526.0 2.5 fusion.24
  528.6 2.6 fusion.30
  532.2 3.7 fusion.17
  535.9 1.9 copy.222
  537.8 162.9 %collective-permute-done.7 = f32[2,2,128,2048]{2,3,1,0:T(8,128)} collective-permute-done((f32[2,2,128,2048]{2,3,1,0:T(8,128)}, f32[2,2,128,2048]{2,3,1,0:T(8,128)}, u32[]{:S(2)}, u32[]{:S(2)}) %collective-permute-start.7) | collective-permute-done | bytes 4194336 | tf_op jit(solution)/shard_map/ppermute | solution.py:137
  700.7 4.4 fusion.14
  (89 shorter events, 24.8 us)
Async XLA Ops:
  11.9 13.7 %all-to-all-start = ((s32[16,1,3]{2,1,0:T(1,128)}), s32[16,1,3]{2,1,0:T(1,128)S(1)}, u32[]{:S(2)}, u32[]{:S(2)}) async-start(s32[16,1,3]{2,1,0:T(1,128)} %copy.159), calls=%async_computation | async-start | bytes 16384 | tf_op jit(solution)/shard_map/all_to_all | solution.py:53
  20.6 1.8 copy-start.7
  22.2 0.8 copy-start.8
  32.5 203.3 %all-to-all-start.1 = ((bf16[16,3,2,128,128]{4,3,2,1,0:T(8,128)(2,1)}), bf16[16,3,2,128,128]{4,3,2,1,0:T(8,128)(2,1)S(1)}, u32[]{:S(2)}, u32[]{:S(2)}) async-start(bf16[16,3,2,128,128]{4,3,2,1,0:T(8,128)(2,1)} %broadcast_select_fusion), calls=%async_computation.1 | async-start | bytes 6291456 | tf_op jit(solution)/shard_map/all_to_all | solution.py:55
  36.3 184.9 %all-reduce.3.cloned.1.call-start = ((), (), s32[]{:S(2)}) async-start(), calls=%async_computation.3 | async-start | bytes 4194304 | tf_op jit(solution)/shard_map/psum | solution.py:26
  38.6 4.9 collective-permute-start
  41.9 13.6 %collective-permute-start.1 = (bf16[2,128,2048]{1,2,0:T(8,128)(2,1)}, bf16[2,128,2048]{1,2,0:T(8,128)(2,1)}, u32[]{:S(2)}, u32[]{:S(2)}) collective-permute-start(bf16[2,128,2048]{1,2,0:T(8,128)(2,1)} %pad_maximum_fusion.5), channel_id=1, source_target_pairs={{1,0},{2,1},{3,2},{4,3},{5,4},{6,5},{7,6},{8,7},{9,8},{10,9},{11,1... | collective-permute-start | bytes 3145736 | tf_op jit(solution)/shard_map/ppermute | solution.py:19
  225.9 6.1 copy-start.10
  230.4 1.6 copy-start
  238.6 2.5 copy-start.5
  238.6 3.6 slice-start.2
  241.0 3.3 copy-start.2
  241.0 2.2 slice-start.3
  244.4 1.1 copy-start.13
  245.5 3.9 copy-start.12
  251.3 4.2 copy-start.11
  254.0 1.5 copy-start.4
  279.8 7.4 %collective-permute-start.4 = (f32[2,2,128,2048]{2,3,1,0:T(8,128)}, f32[2,2,128,2048]{2,3,1,0:T(8,128)S(1)}, u32[]{:S(2)}, u32[]{:S(2)}) collective-permute-start(f32[2,2,128,2048]{2,3,1,0:T(8,128)} %bitcast.159), channel_id=1, source_target_pairs={{0,1},{1,0},{2,3},{3,2},{4,5},{5,4},{6,7},{7,6},{8,9},{9,8},{10,11... | collective-permute-start | bytes 12582920 | tf_op jit(solution)/shard_map/ppermute | solution.py:137
  290.0 96.7 %copy-start.3 = (bf16[48,2,128,128]{3,2,0,1:T(8,128)(2,1)S(1)}, bf16[48,2,128,128]{3,2,0,1:T(8,128)(2,1)}, u32[]{:S(2)}) copy-start(bf16[48,2,128,128]{3,2,0,1:T(8,128)(2,1)} %copy-done.2) | copy-start | bytes 9437188
  290.0 96.7 %copy-start.14 = (bf16[128,2048]{0,1:T(8,128)(2,1)S(1)}, bf16[128,2048]{0,1:T(8,128)(2,1)}, u32[]{:S(2)}) copy-start(bf16[128,2048]{0,1:T(8,128)(2,1)} %copy.168) | copy-start | bytes 1572868
  290.0 92.7 %collective-permute-start.5 = (f32[2,2,128,2048]{2,3,1,0:T(8,128)S(1)}, f32[2,2,128,2048]{2,3,1,0:T(8,128)S(1)}, u32[]{:S(2)}, u32[]{:S(2)}) collective-permute-start(f32[2,2,128,2048]{2,3,1,0:T(8,128)S(1)} %bitcast_add_fusion), channel_id=1, source_target_pairs={{0,2},{1,3},{2,0},{3,1},{4,6},{5,7},{6,4},{7,5},{8,10},{9,11},{10,... | collective-permute-start | bytes 12582920 | tf_op jit(solution)/shard_map/ppermute | solution.py:137
  385.1 126.0 %collective-permute-start.6 = (f32[2,2,128,2048]{2,3,1,0:T(8,128)}, f32[2,2,128,2048]{2,3,1,0:T(8,128)}, u32[]{:S(2)}, u32[]{:S(2)}) collective-permute-start(f32[2,2,128,2048]{2,3,1,0:T(8,128)} %add.86), channel_id=1, source_target_pairs={{0,4},{1,5},{2,6},{3,7},{4,0},{5,1},{6,2},{7,3},{8,12},{9,13},{10,... | collective-permute-start | bytes 12582920 | tf_op jit(solution)/shard_map/ppermute | solution.py:137
  386.7 2.1 copy-start.6
  387.7 1.1 copy-start.9
  401.5 115.5 %slice-start = ((s8[5242880]{0:T(1024)(128)(4,1)}), s8[1048576]{0:T(1024)(128)(4,1)S(1)}, s32[]{:S(2)}) async-start(s8[5242880]{0:T(1024)(128)(4,1)} %bitcast.149), calls=%async_computation.4 | async-start | bytes 2097152
  401.5 130.7 %all-to-all-start.2 = ((bf16[16,3,2,128,128]{4,3,2,1,0:T(8,128)(2,1)}), bf16[16,3,2,128,128]{4,3,2,1,0:T(8,128)(2,1)}, u32[]{:S(2)}, u32[]{:S(2)}) async-start(bf16[16,3,2,128,128]{4,3,2,1,0:T(8,128)(2,1)} %scatter_fusion.1), calls=%async_computation.2 | async-start | bytes 6291456 | tf_op jit(solution)/shard_map/all_to_all | solution.py:158
  406.1 110.9 %slice-start.1 = ((s8[5242880]{0:T(1024)(128)(4,1)}), s8[4194304]{0:T(1024)(128)(4,1)S(1)}, s32[]{:S(2)}) async-start(s8[5242880]{0:T(1024)(128)(4,1)} %bitcast.149), calls=%async_computation.5 | async-start | bytes 8388608
  517.0 183.7 %collective-permute-start.7 = (f32[2,2,128,2048]{2,3,1,0:T(8,128)}, f32[2,2,128,2048]{2,3,1,0:T(8,128)}, u32[]{:S(2)}, u32[]{:S(2)}) collective-permute-start(f32[2,2,128,2048]{2,3,1,0:T(8,128)} %add.87), channel_id=1, source_target_pairs={{0,8},{1,9},{2,10},{3,11},{4,12},{5,13},{6,14},{7,15},{8,0},{9,1},... | collective-permute-start | bytes 12582920 | tf_op jit(solution)/shard_map/ppermute | solution.py:137
  521.9 6.6 copy-start.1
  521.9 15.9 %collective-permute-start.2 = (bf16[2,128,2048]{1,2,0:T(8,128)(2,1)}, bf16[2,128,2048]{1,2,0:T(8,128)(2,1)}, u32[]{:S(2)}, u32[]{:S(2)}) collective-permute-start(bf16[2,128,2048]{1,2,0:T(8,128)(2,1)} %get-tuple-element.22), channel_id=1, source_target_pairs={{0,1},{1,2},{2,3},{3,4},{4,5},{5,6},{6,7},{7,8},{8,9},{9,10},{10,1... | collective-permute-start | bytes 3145736 | tf_op jit(solution)/shard_map/ppermute | solution.py:18
  524.4 13.4 %collective-permute-start.3 = (bf16[2,128,2048]{1,2,0:T(8,128)(2,1)}, bf16[2,128,2048]{1,2,0:T(8,128)(2,1)}, u32[]{:S(2)}, u32[]{:S(2)}) collective-permute-start(bf16[2,128,2048]{1,2,0:T(8,128)(2,1)} %get-tuple-element.23), channel_id=1, source_target_pairs={{1,0},{2,1},{3,2},{4,3},{5,4},{6,5},{7,6},{8,7},{9,8},{10,9},{11,1... | collective-permute-start | bytes 3145736 | tf_op jit(solution)/shard_map/ppermute | solution.py:19
Sparse Core Ops, SparseCore 0:
  49.4 171.7 all-reduce.2
